TPU v7x, 256 devices: a whole 4x4x8 slice. The times are simulated.
256 devices in a mesh: tok: 64 (over x, z, core), head: 4 (over y).
Axes of the slice: x: 4, y: 4, z: 8, core: 2. Of those that a mesh axis runs over, the one named last changes fastest.
Arguments:
- queries: bfloat16 [2, 8192, 2048], P(None, 'tok', 'head'), may hold values from -16 to 16
- keys: bfloat16 [8192, 2048], P('tok', 'head'), may hold values from -16 to 16
- values: bfloat16 [8192, 2048], P('tok', 'head'), may hold values from -6 to 6
- upstream: bfloat16 [2, 8192, 2048], P(None, 'tok', 'head'), may hold values from -6 to 6
- out_gain: float32 [2048], P('head'), may hold values from 0.5 to 2
- gate_weight: bfloat16 [4, 512, 512], P('head', 'tok'), may hold values from -0.25 to 0.25
- up_weight: bfloat16 [4, 512, 512], P('head', 'tok'), may hold values from -0.25 to 0.25
- down_weight: bfloat16 [4, 512, 512], P('head', 'tok'), may hold values from -0.25 to 0.25
Outputs:
- grad_queries: bfloat16 [2, 8192, 2048], P(None, 'tok', 'head')
- grad_keys: bfloat16 [8192, 2048], P('tok', 'head')
- grad_values: bfloat16 [8192, 2048], P('tok', 'head')
- grad_gate: float32 [4, 512, 512], P('head', 'tok')
- grad_up: float32 [4, 512, 512], P('head', 'tok')
- grad_down: float32 [4, 512, 512], P('head', 'tok')
All inputs are finite; a program needn't handle non-finite values.
Results may differ from a plain program's by a relative error of at most 0.02.
Values may be sent and summed in bfloat16 or wider, within the bound.
A program may use at most 128 MiB of HBM per device.

v0:
```python
import math
import jax
import jax.numpy as jnp
from jax import lax
from jax.sharding import PartitionSpec as P

NS_STEPS = 2
lin_coef = 3.4445
cube_coef = -4.775
fifth_coef = 2.0315
rms_eps = 1e-06
fro_eps = 1e-07


def product(left, right):
    return jnp.dot(left, right, preferred_element_type=jnp.float32)


def across(left, right):
    return lax.dot_general(
        left, right, (((0,), (0,)), ((), ())), preferred_element_type=jnp.float32
    )


def against(left, right):
    return lax.dot_general(
        left, right, (((1,), (1,)), ((), ())), preferred_element_type=jnp.float32
    )


def fast_forward(keys, values, weights):
    gate_weight, up_weight, down_weight = weights
    gate_pre = product(keys, gate_weight)
    up_pre = product(keys, up_weight)
    sigma = jax.nn.sigmoid(gate_pre)
    active = gate_pre * sigma
    hidden = (active * up_pre).astype(jnp.bfloat16)
    back = -against(values, down_weight)
    slope = sigma * (1.0 + gate_pre * (1.0 - sigma))
    d_gate = (back * up_pre * slope).astype(jnp.bfloat16)
    d_up = (back * active).astype(jnp.bfloat16)
    fast = (across(keys, d_gate), across(keys, d_up), -across(hidden, values))
    saved = (gate_pre, up_pre, sigma, active, hidden, back, slope, d_gate, d_up)
    return (fast, saved)


def fast_second(keys, values, weights, saved, cots):
    gate_weight, up_weight, down_weight = weights
    gate_pre, up_pre, sigma, active, hidden, back, slope, d_gate, d_up = saved
    cot_gate, cot_up, cot_down = cots
    along_gate = product(keys, cot_gate)
    along_up = product(keys, cot_up)
    along_hidden = -against(values, cot_down)
    curve = sigma * (1.0 - sigma) * (2.0 + gate_pre * (1.0 - 2.0 * sigma))
    d_back = (along_gate * up_pre * slope + along_up * active).astype(jnp.bfloat16)
    d_upper = (along_gate * back * slope + along_hidden * active).astype(jnp.bfloat16)
    d_lower = (
        along_gate * back * up_pre * curve + along_up * back * slope + along_hidden * up_pre * slope
    ).astype(jnp.bfloat16)
    grad_keys = (
        against(d_gate, cot_gate)
        + against(d_up, cot_up)
        + against(d_lower, gate_weight)
        + against(d_upper, up_weight)
    ).astype(jnp.bfloat16)
    grad_values = (-product(hidden, cot_down) - product(d_back, down_weight)).astype(jnp.bfloat16)
    partial_value = (across(keys, d_lower), across(keys, d_upper), -across(d_back, values))
    return (grad_keys, grad_values, partial_value)


def apply_forward(queries, weights):
    gate_weight, up_weight, down_weight = weights
    gate_pre = product(queries, gate_weight)
    up_pre = product(queries, up_weight)
    sigma = jax.nn.sigmoid(gate_pre)
    hidden = (gate_pre * sigma * up_pre).astype(jnp.bfloat16)
    output = product(hidden, down_weight)
    return (gate_pre, up_pre, sigma, hidden, output)


def statistics(output, upstream, out_gain, width):
    weighted = out_gain * upstream.astype(jnp.float32)
    sums = lax.psum((jnp.sum(output * output, axis=1), jnp.sum(weighted * output, axis=1)), "head")
    return (lax.rsqrt(sums[0] / width + rms_eps), sums[1] / width)


def apply_backward(queries, weights, saved, upstream, out_gain, width):
    gate_weight, up_weight, down_weight = weights
    gate_pre, up_pre, sigma, hidden, output = saved
    inverse_rms, mean_dot = statistics(output, upstream, out_gain, width)
    weighted = out_gain * upstream.astype(jnp.float32)
    d_output = (
        inverse_rms[:, None] * weighted
        - output * (inverse_rms * inverse_rms * inverse_rms * mean_dot)[:, None]
    ).astype(jnp.bfloat16)
    back = against(d_output, down_weight)
    slope = sigma * (1.0 + gate_pre * (1.0 - sigma))
    d_gate = (back * up_pre * slope).astype(jnp.bfloat16)
    d_up = (back * gate_pre * sigma).astype(jnp.bfloat16)
    grad_queries = (against(d_gate, gate_weight) + against(d_up, up_weight)).astype(jnp.bfloat16)
    partial_value = (across(queries, d_gate), across(queries, d_up), across(hidden, d_output))
    return (grad_queries, partial_value)


def schulz_forward(begin):
    current = begin
    saved = []
    for sweep in range(NS_STEPS):
        gram = against(current, current).astype(jnp.bfloat16)
        blend = (cube_coef * gram.astype(jnp.float32) + fifth_coef * product(gram, gram)).astype(
            jnp.bfloat16
        )
        following = (lin_coef * current.astype(jnp.float32) + product(blend, current)).astype(
            jnp.bfloat16
        )
        saved.append((current, gram, blend))
        current = following
    return (current, saved)


def schulz_backward(cotan, saved):
    current = cotan
    for iterate, gram, blend in reversed(saved):
        cross = against(current, iterate)
        symmetric = (cross + cross.T).astype(jnp.bfloat16)
        bent = product(symmetric, gram)
        mixed = (cube_coef * symmetric.astype(jnp.float32) + fifth_coef * (bent + bent.T)).astype(
            jnp.bfloat16
        )
        current = (
            lin_coef * current.astype(jnp.float32)
            + product(blend, current)
            + product(mixed, iterate)
        ).astype(jnp.bfloat16)
    return current


def per_device(queries, keys, values, upstream, out_gain, gate_weight, up_weight, down_weight):
    shards = lax.axis_size("tok")
    owner = lax.axis_index("tok")
    width = out_gain.shape[0] * lax.axis_size("head")
    scale = 1.0 / math.sqrt(queries.shape[1] * shards)
    own_rows = (gate_weight[0], up_weight[0], down_weight[0])
    starts = [owner * own_rows[which].shape[0] for which in range(3)]
    first = (
        lax.all_gather(own_rows[0], "tok", axis=0, tiled=True),
        lax.all_gather(own_rows[1], "tok", axis=0, tiled=True),
        lax.all_gather(own_rows[2], "tok", axis=0, tiled=True),
    )
    fast, saved_keys = fast_forward(keys, values, first)
    apply_first = apply_forward(queries[0], first)
    grad_first, partial_first = apply_backward(
        queries[0], first, apply_first, upstream[0], out_gain, width
    )
    totals = lax.psum((fast[0], fast[1], fast[2]), "tok")
    roots = [jnp.sqrt(jnp.sum(totals[which] * totals[which])) for which in range(3)]
    forward = [
        schulz_forward((totals[which] / (roots[which] + fro_eps)).astype(jnp.bfloat16))
        for which in range(3)
    ]
    finals = [forward[which][0] for which in range(3)]
    second = tuple(
        (
            (first[which].astype(jnp.float32) - finals[which].astype(jnp.float32)).astype(
                jnp.bfloat16
            )
            for which in range(3)
        )
    )
    apply_second = apply_forward(queries[1], second)
    grad_second, partial_second = apply_backward(
        queries[1], second, apply_second, upstream[1], out_gain, width
    )
    rates = lax.psum((partial_second[0], partial_second[1], partial_second[2]), "tok")
    bottoms = [
        schulz_backward((-rates[which]).astype(jnp.bfloat16), forward[which][1])
        for which in range(3)
    ]
    cots = []
    for which in range(3):
        norm = roots[which] + fro_eps
        inner = jnp.sum(bottoms[which].astype(jnp.float32) * totals[which])
        cots.append(
            (
                bottoms[which].astype(jnp.float32) / norm
                - totals[which] * (inner / (norm * norm * roots[which]))
            ).astype(jnp.bfloat16)
        )
    rate_rows = [
        lax.dynamic_slice_in_dim(rates[which], starts[which], own_rows[which].shape[0], 0)
        for which in range(3)
    ]
    grad_keys, grad_values, second_order = fast_second(keys, values, first, saved_keys, cots)
    sums = (
        lax.psum_scatter(
            partial_first[0] + second_order[0], "tok", scatter_dimension=0, tiled=True
        ),
        lax.psum_scatter(
            partial_first[1] + second_order[1], "tok", scatter_dimension=0, tiled=True
        ),
        lax.psum_scatter(
            partial_first[2] + second_order[2], "tok", scatter_dimension=0, tiled=True
        ),
    )
    grad_gate = ((sums[0] + rate_rows[0]) * scale)[None]
    grad_up = ((sums[1] + rate_rows[1]) * scale)[None]
    grad_down = ((sums[2] + rate_rows[2]) * scale)[None]
    grad_queries = jnp.stack([grad_first, grad_second])
    return (grad_queries, grad_keys, grad_values, grad_gate, grad_up, grad_down)


def solution(mesh):
    in_specs = (
        P(None, "tok", "head"),
        P("tok", "head"),
        P("tok", "head"),
        P(None, "tok", "head"),
        P("head"),
        P("head", "tok", None),
        P("head", "tok", None),
        P("head", "tok", None),
    )
    out_specs = (
        P(None, "tok", "head"),
        P("tok", "head"),
        P("tok", "head"),
        P("head", "tok", None),
        P("head", "tok", None),
        P("head", "tok", None),
    )
    return jax.shard_map(
        per_device, mesh=mesh, in_specs=in_specs, out_specs=out_specs, check_vma=False
    )
```

profile of v0, /device:TPU:8, one launch (start us, length us, event | category | flops | bytes accessed | tf_op | source)
XLA Modules:
  0.0 1135.4 jit_solution(10835314642906359188)
XLA Ops:
  7.2 53.5 %all-gather = bf16[1,512,512]{2,1,0:T(8,128)(2,1)S(1)} all-gather(bf16[1,8,512]{2,1,0:T(8,128)(2,1)} %param.13), channel_id=2, replica_groups=mesh['tok'=64,'head'=4] {'tok'}, dimensions={1}, use_global_device_ids=true | all-gather | bytes 532480 | tf_op jit(solution)/shard_map/all_gather | solution.py:146
  60.8 49.5 %all-gather.2 = bf16[1,512,512]{2,1,0:T(8,128)(2,1)S(1)} all-gather(bf16[1,8,512]{2,1,0:T(8,128)(2,1)S(1)} %copy-done.104), channel_id=4, replica_groups=mesh['tok'=64,'head'=4] {'tok'}, dimensions={1}, use_global_device_ids=true | all-gather | bytes 532480 | tf_op jit(solution)/shard_map/all_gather | solution.py:148
  110.2 48.1 %all-gather.1 = bf16[1,512,512]{2,1,0:T(8,128)(2,1)S(1)} all-gather(bf16[1,8,512]{2,1,0:T(8,128)(2,1)S(1)} %copy-done.105), channel_id=3, replica_groups=mesh['tok'=64,'head'=4] {'tok'}, dimensions={1}, use_global_device_ids=true | all-gather | bytes 532480 | tf_op jit(solution)/shard_map/all_gather | solution.py:147
  169.9 186.9 %all-reduce.8.cloned.1.call-done = (f32[512,512]{0,1:T(8,128)}, f32[512,512]{0,1:T(8,128)}, f32[512,512]{0,1:T(8,128)}) async-done(((f32[512,512]{0,1:T(8,128)}, f32[512,512]{0,1:T(8,128)}, f32[512,512]{0,1:T(8,128)}), (f32[512,512]{0,1:T(8,128)}, f32[512,512]{0,1:T(8,128)}, f32[512,512]{0,1:T(8,128)})) %all-reduce.8.cloned.1.call-update) | async-done | bytes 3145744 | tf_op jit(solution)/shard_map/psum | solution.py:155
  356.8 2.2 multiply_reduce_fusion.2
  384.9 1.5 fusion.129
  386.3 9.2 all-reduce.2
  396.2 2.0 fusion.128
  402.8 2.1 multiply_convert_fusion.6
  406.8 188.1 %all-reduce.6.cloned.1.call-done = (f32[512,512]{0,1:T(8,128)}, f32[512,512]{0,1:T(8,128)}, f32[512,512]{0,1:T(8,128)}) async-done(((f32[512,512]{0,1:T(8,128)}, f32[512,512]{0,1:T(8,128)}, f32[512,512]{0,1:T(8,128)}), (f32[512,512]{0,1:T(8,128)}, f32[512,512]{0,1:T(8,128)}, f32[512,512]{0,1:T(8,128)})) %all-reduce.6.cloned.1.call-update) | async-done | bytes 3145744 | tf_op jit(solution)/shard_map/psum | solution.py:174
  594.9 3.3 convolution_add_fusion.13
  598.2 1.4 fusion.131
  599.7 2.6 copy.72
  602.3 1.8 fusion.75
  606.2 2.6 copy.73
  608.8 2.7 fusion.30
  611.6 1.5 convolution_add_fusion.11
  613.0 1.5 fusion.169
  614.5 1.5 convolution_add_fusion.9
  616.0 1.4 fusion.132
  617.4 2.6 copy.80
  620.0 1.8 fusion.67
  624.0 2.6 copy.81
  626.5 2.7 fusion.32
  632.2 1.5 convolution_add_fusion.5
  633.7 1.4 fusion.133
  635.1 2.6 copy.91
  637.7 1.8 fusion.59
  641.7 2.6 copy.92
  644.2 2.7 fusion.34
  647.0 1.5 convolution_add_fusion.3
  648.5 1.5 fusion.177
  650.0 2.5 copy.76
  652.5 1.8 fusion.71
  656.5 2.5 copy.77
  659.1 2.6 copy.84
  661.6 1.8 fusion.63
  665.6 2.6 copy.85
  668.2 4.1 fusion.45
  672.9 4.4 fusion.48
  678.0 2.9 fusion.44
  682.8 2.6 copy.95
  689.3 3.8 fusion.51
  699.4 2.5 copy.128
  704.4 2.5 copy.130
  720.7 120.6 %reduce-scatter.10.cloned.1.call-done = f32[8,512]{1,0:T(8,128)} async-done(((f32[512,512]{1,0:T(8,128)}), f32[8,512]{1,0:T(8,128)}) %reduce-scatter.10.cloned.1.call-update) | async-done | bytes 16400
  843.9 139.7 %reduce-scatter.12.cloned.1.call-done = f32[8,512]{1,0:T(8,128)} async-done(((f32[512,512]{1,0:T(8,128)}), f32[8,512]{1,0:T(8,128)}) %reduce-scatter.12.cloned.1.call-update) | async-done | bytes 16400
  986.3 139.7 %reduce-scatter.14.cloned.1.call-done = f32[8,512]{1,0:T(8,128)} async-done(((f32[512,512]{1,0:T(8,128)}), f32[8,512]{1,0:T(8,128)}) %reduce-scatter.14.cloned.1.call-update) | async-done | bytes 16400
  (313 shorter events, 91.4 us)
Async XLA Ops:
  7.2 151.2 %copy-start = (bf16[128,512]{1,0:T(8,128)(2,1)S(1)}, bf16[128,512]{1,0:T(8,128)(2,1)}, u32[]{:S(2)}) copy-start(bf16[128,512]{1,0:T(8,128)(2,1)} %param.9) | copy-start | bytes 393220
  7.2 53.6 %copy-start.104 = (bf16[1,8,512]{2,1,0:T(8,128)(2,1)S(1)}, bf16[1,8,512]{2,1,0:T(8,128)(2,1)}, u32[]{:S(2)}) copy-start(bf16[1,8,512]{2,1,0:T(8,128)(2,1)} %param.15) | copy-start | bytes 24580
  7.2 349.6 %all-reduce.8.cloned.1.call-start = ((), (), s32[]{:S(2)}) async-start(), calls=%async_computation.7 | async-start | bytes 6291456 | tf_op jit(solution)/shard_map/psum | solution.py:155
  60.8 49.5 %copy-start.105 = (bf16[1,8,512]{2,1,0:T(8,128)(2,1)S(1)}, bf16[1,8,512]{2,1,0:T(8,128)(2,1)}, u32[]{:S(2)}) copy-start(bf16[1,8,512]{2,1,0:T(8,128)(2,1)} %param.14) | copy-start | bytes 24580
  158.4 10.5 copy-start.5
  161.0 1.4 copy-start.46
  161.0 2.7 copy-start.48
  165.1 429.9 %all-reduce.6.cloned.1.call-start = ((), (), s32[]{:S(2)}) async-start(), calls=%async_computation.6 | async-start | bytes 6291456 | tf_op jit(solution)/shard_map/psum | solution.py:174
  356.8 2.9 copy-start.2
  361.9 1.7 copy-start.31
  364.2 2.6 copy-start.3
  368.5 1.7 copy-start.20
  372.3 1.5 copy-start.1
  375.5 1.8 copy-start.16
  378.1 4.8 copy-start.26
  380.8 2.1 copy-start.41
  383.7 2.6 copy-start.60
  384.2 2.1 copy-start.40
  396.2 2.0 copy-start.59
  402.5 438.7 %reduce-scatter.10.cloned.1.call-start = ((), (), s32[]{:S(2)}) async-start(), calls=%async_computation.3 | async-start | bytes 1064960
  594.9 3.3 copy-start.9
  594.9 3.3 copy-start.32
  602.3 2.6 copy-start.84
  608.8 2.7 copy-start.80
  611.5 1.5 copy-start.19
  613.0 1.5 copy-start.8
  613.0 1.5 copy-start.44
  614.5 1.5 copy-start.30
  620.0 2.6 copy-start.82
  626.5 2.7 copy-start.76
  629.3 1.4 copy-start.21
  630.7 1.4 copy-start.7
  630.7 1.4 copy-start.42
  632.2 1.5 copy-start.27
  637.7 2.6 copy-start.78
  644.2 2.7 copy-start.74
  647.0 1.5 copy-start.17
  652.5 2.6 copy-start.70
  661.6 2.5 copy-start.72
  682.8 2.6 copy-start.4
  685.4 2.2 copy-start.68
  693.8 1.6 copy-start.96
  693.8 1.6 copy-start.100
  693.8 1.6 copy-start.108
  696.3 1.8 copy-start.24
  697.4 5.7 copy-start.91
  701.9 281.7 %reduce-scatter.12.cloned.1.call-start = ((), (), s32[]{:S(2)}) async-start(), calls=%async_computation.4 | async-start | bytes 1064960
  707.0 419.0 %reduce-scatter.14.cloned.1.call-start = ((), (), s32[]{:S(2)}) async-start(), calls=%async_computation.5 | async-start | bytes 1064960
  (67 other events, 65.9 us)
Sparse Core Ops, SparseCore 0:
  165.2 191.5 all-reduce.7
  402.7 192.2 all-reduce.5
  702.1 139.1 reduce-scatter.9
  845.1 138.5 reduce-scatter.11
  987.5 138.5 reduce-scatter.13
where the time goes:
time: 1140 us
  waiting for transfers between devices  775 us (68%)
  blocking collectives  160 us (14%)
  matrix products  85.5 us (8%)
  local copies, waits for them, and re-layouts  69.9 us (6%)
  other arithmetic  24.7 us (2%)
  between operations  19 us (2%)
    unnamed x8, waiting for transfers between devices  400 us
    psum x1, waiting for transfers between devices, per_device(): lax.psum((partial_second[0], partial_second[1], partial_second[2]), 'tok')  188 us
    psum x1, waiting for transfers between devices, per_device(): totals = lax.psum((fast[0], fast[1], fast[2]), 'tok')  187 us
    dot_general x42, matrix products, product(): return jnp.dot(left, right, preferred_element_type=jnp.float32)  54.5 us
    all_gather x1, blocking collectives, per_device(): lax.all_gather(own_rows[0], 'tok', axis=0, tiled=True)  53.5 us
    all_gather x1, blocking collectives, per_device(): lax.all_gather(own_rows[2], 'tok', axis=0, tiled=True)  49.5 us
    all_gather x1, blocking collectives, per_device(): lax.all_gather(own_rows[1], 'tok', axis=0, tiled=True)  48.1 us
    unnamed x228, local copies, waits for them, and re-layouts  37.3 us
  transfers between devices with their start and end apart: 5, of which 5 were waited for; matrix products, arithmetic and copies ran while one was open for 2% of the time, Pallas kernels for 0%

commit v1 on v0

--- a/solution.py
+++ b/solution.py
@@ -143,7 +143,9 @@
     own_rows = (gate_weight[0], up_weight[0], down_weight[0])
     starts = [owner * own_rows[which].shape[0] for which in range(3)]
     first = (
-        lax.all_gather(own_rows[0], "tok", axis=0, tiled=True),
+        jnp.concatenate(
+            lax.all_to_all(jnp.stack([own_rows[0]] * lax.axis_size("tok")), "tok", 0, 0), axis=0
+        ),
         lax.all_gather(own_rows[1], "tok", axis=0, tiled=True),
         lax.all_gather(own_rows[2], "tok", axis=0, tiled=True),
     )

time: 1140 us -> 1110 us (0.974)
  blocking collectives: 160 us -> 116 us
  starting transfers between devices: 0.84 us -> 12.7 us
    all_gather x1 -> x0, blocking collectives: 53.5 us -> none  [per_device(): lax.all_gather(own_rows[0], 'tok', axis=0, tiled=True)]
    all_to_all x0 -> x1, starting transfers between devices: none -> 12.1 us  [per_device(): lax.all_to_all(jnp.stack([own_rows[0]] * lax.axis_size('tok')), 'tok', 0, 0)]
  transfers between devices with their start and end apart: 5 -> 6, of which waited for: 5 -> 5; matrix products, arithmetic and copies ran while one was open for 2% -> 2% of each run, Pallas kernels for 0% -> 0%
where the time goes in v1:
time: 1110 us; the launch traced here: 1100 us
  waiting for transfers between devices  776 us (70%)
  blocking collectives  116 us (10%)
  matrix products  85.4 us (8%)
  local copies, waits for them, and re-layouts  70.8 us (6%)
  other arithmetic  24.7 us (2%)
  between operations  18.8 us (2%)
  starting transfers between devices  12.7 us (1%)
    unnamed x8, waiting for transfers between devices  400 us
    psum x1, waiting for transfers between devices, per_device(): lax.psum((partial_second[0], partial_second[1], partial_second[2]), 'tok')  188 us
    psum x1, waiting for transfers between devices, per_device(): totals = lax.psum((fast[0], fast[1], fast[2]), 'tok')  187 us
    all_gather x1, blocking collectives, per_device(): lax.all_gather(own_rows[2], 'tok', axis=0, tiled=True)  57.5 us
    dot_general x42, matrix products, product(): return jnp.dot(left, right, preferred_element_type=jnp.float32)  54.5 us
    all_gather x1, blocking collectives, per_device(): lax.all_gather(own_rows[1], 'tok', axis=0, tiled=True)  49.6 us
    unnamed x228, local copies, waits for them, and re-layouts  36.6 us
  transfers between devices with their start and end apart: 6, of which 5 were waited for; matrix products, arithmetic and copies ran while one was open for 2% of the time, Pallas kernels for 0%

profile of v1, /device:TPU:8, one launch (start us, length us, event | category | flops | bytes accessed | tf_op | source)
XLA Modules:
  0.0 1104.6 jit_solution(12973535871493212892)
XLA Ops:
  7.2 1.6 stack.12
  8.7 12.1 %all-to-all-start = ((bf16[64,8,512]{2,1,0:T(8,128)(2,1)}), bf16[64,8,512]{2,1,0:T(8,128)(2,1)S(1)}, u32[]{:S(2)}, u32[]{:S(2)}) async-start(bf16[64,8,512]{2,1,0:T(8,128)(2,1)} %stack.12), calls=%async_computation | async-start | bytes 1048576 | tf_op jit(solution)/shard_map/all_to_all | solution.py:147
  20.9 57.5 %all-gather.1 = bf16[1,512,512]{2,1,0:T(8,128)(2,1)S(1)} all-gather(bf16[1,8,512]{2,1,0:T(8,128)(2,1)S(1)} %copy-done.104), channel_id=3, replica_groups=mesh['tok'=64,'head'=4] {'tok'}, dimensions={1}, use_global_device_ids=true | all-gather | bytes 532480 | tf_op jit(solution)/shard_map/all_gather | solution.py:150
  78.4 49.6 %all-gather = bf16[1,512,512]{2,1,0:T(8,128)(2,1)S(1)} all-gather(bf16[1,8,512]{2,1,0:T(8,128)(2,1)S(1)} %copy-done.105), channel_id=2, replica_groups=mesh['tok'=64,'head'=4] {'tok'}, dimensions={1}, use_global_device_ids=true | all-gather | bytes 532480 | tf_op jit(solution)/shard_map/all_gather | solution.py:149
  138.5 187.4 %all-reduce.8.cloned.1.call-done = (f32[512,512]{0,1:T(8,128)}, f32[512,512]{0,1:T(8,128)}, f32[512,512]{0,1:T(8,128)}) async-done(((f32[512,512]{0,1:T(8,128)}, f32[512,512]{0,1:T(8,128)}, f32[512,512]{0,1:T(8,128)}), (f32[512,512]{0,1:T(8,128)}, f32[512,512]{0,1:T(8,128)}, f32[512,512]{0,1:T(8,128)})) %all-reduce.8.cloned.1.call-update) | async-done | bytes 3145744 | tf_op jit(solution)/shard_map/psum | solution.py:157
  325.9 2.2 multiply_reduce_fusion.2
  354.0 1.5 fusion.122
  355.5 9.2 all-reduce.2
  365.4 2.0 fusion.121
  372.0 2.1 multiply_convert_fusion.6
  376.0 188.4 %all-reduce.6.cloned.1.call-done = (f32[512,512]{0,1:T(8,128)}, f32[512,512]{0,1:T(8,128)}, f32[512,512]{0,1:T(8,128)}) async-done(((f32[512,512]{0,1:T(8,128)}, f32[512,512]{0,1:T(8,128)}, f32[512,512]{0,1:T(8,128)}), (f32[512,512]{0,1:T(8,128)}, f32[512,512]{0,1:T(8,128)}, f32[512,512]{0,1:T(8,128)})) %all-reduce.6.cloned.1.call-update) | async-done | bytes 3145744 | tf_op jit(solution)/shard_map/psum | solution.py:176
  564.4 3.3 convolution_add_fusion.13
  569.1 2.6 copy.117
  571.7 1.8 fusion.75
  575.6 2.6 copy.118
  578.2 2.7 fusion.30
  581.0 1.4 convolution_add_fusion.11
  582.4 1.4 fusion.169
  583.9 1.5 convolution_add_fusion.9
  586.8 2.6 copy.125
  589.4 1.8 fusion.67
  593.4 2.6 copy.126
  595.9 2.7 fusion.32
  598.7 1.4 convolution_add_fusion.7
  601.6 1.5 convolution_add_fusion.5
  604.5 2.6 copy.136
  607.1 1.8 fusion.59
  611.1 2.6 copy.137
  613.6 2.7 fusion.34
  616.4 1.5 convolution_add_fusion.3
  617.9 1.5 fusion.177
  619.4 2.5 copy.121
  621.9 1.8 fusion.71
  625.9 2.5 copy.122
  628.4 2.6 copy.129
  631.0 1.8 fusion.63
  633.5 1.4 fusion.174
  635.0 2.6 copy.130
  637.5 4.1 fusion.45
  642.3 4.4 fusion.48
  647.4 3.0 fusion.44
  652.2 2.6 copy.140
  658.8 3.8 fusion.51
  668.8 2.5 copy.173
  673.8 2.5 copy.175
  690.1 120.6 %reduce-scatter.10.cloned.1.call-done = f32[8,512]{1,0:T(8,128)} async-done(((f32[512,512]{1,0:T(8,128)}), f32[8,512]{1,0:T(8,128)}) %reduce-scatter.10.cloned.1.call-update) | async-done | bytes 16400
  813.3 139.8 %reduce-scatter.12.cloned.1.call-done = f32[8,512]{1,0:T(8,128)} async-done(((f32[512,512]{1,0:T(8,128)}), f32[8,512]{1,0:T(8,128)}) %reduce-scatter.12.cloned.1.call-update) | async-done | bytes 16400
  955.7 139.7 %reduce-scatter.14.cloned.1.call-done = f32[8,512]{1,0:T(8,128)} async-done(((f32[512,512]{1,0:T(8,128)}), f32[8,512]{1,0:T(8,128)}) %reduce-scatter.14.cloned.1.call-update) | async-done | bytes 16400
  (315 shorter events, 91.8 us)
Async XLA Ops:
  7.2 121.2 %copy-start = (bf16[128,512]{1,0:T(8,128)(2,1)S(1)}, bf16[128,512]{1,0:T(8,128)(2,1)}, u32[]{:S(2)}) copy-start(bf16[128,512]{1,0:T(8,128)(2,1)} %param.9) | copy-start | bytes 393220
  8.7 12.1 %copy-start.104 = (bf16[1,8,512]{2,1,0:T(8,128)(2,1)S(1)}, bf16[1,8,512]{2,1,0:T(8,128)(2,1)}, u32[]{:S(2)}) copy-start(bf16[1,8,512]{2,1,0:T(8,128)(2,1)} %param.15) | copy-start | bytes 24580
  8.7 119.6 %all-to-all-start = ((bf16[64,8,512]{2,1,0:T(8,128)(2,1)}), bf16[64,8,512]{2,1,0:T(8,128)(2,1)S(1)}, u32[]{:S(2)}, u32[]{:S(2)}) async-start(bf16[64,8,512]{2,1,0:T(8,128)(2,1)} %stack.12), calls=%async_computation | async-start | bytes 1048576 | tf_op jit(solution)/shard_map/all_to_all | solution.py:147
  20.8 57.6 %copy-start.105 = (bf16[1,8,512]{2,1,0:T(8,128)(2,1)S(1)}, bf16[1,8,512]{2,1,0:T(8,128)(2,1)}, u32[]{:S(2)}) copy-start(bf16[1,8,512]{2,1,0:T(8,128)(2,1)} %param.14) | copy-start | bytes 24580
  20.8 305.1 %all-reduce.8.cloned.1.call-start = ((), (), s32[]{:S(2)}) async-start(), calls=%async_computation.8 | async-start | bytes 6291456 | tf_op jit(solution)/shard_map/psum | solution.py:157
  78.4 49.6 %copy-start.33 = (bf16[128,512]{1,0:T(8,128)(2,1)S(1)}, bf16[128,512]{1,0:T(8,128)(2,1)}, u32[]{:S(2)}) copy-start(bf16[128,512]{1,0:T(8,128)(2,1)} %param.10) | copy-start | bytes 393220
  128.0 9.5 copy-start.5
  130.0 2.7 copy-start.48
  134.0 430.4 %all-reduce.6.cloned.1.call-start = ((), (), s32[]{:S(2)}) async-start(), calls=%async_computation.7 | async-start | bytes 6291456 | tf_op jit(solution)/shard_map/psum | solution.py:176
  325.9 2.9 copy-start.2
  331.1 1.7 copy-start.31
  333.4 2.6 copy-start.3
  337.7 1.7 copy-start.20
  341.5 1.5 copy-start.1
  344.7 1.7 copy-start.16
  347.3 4.8 copy-start.26
  350.0 2.1 copy-start.41
  352.9 2.7 copy-start.60
  353.3 2.2 copy-start.40
  365.4 2.0 copy-start.59
  371.7 439.0 %reduce-scatter.10.cloned.1.call-start = ((), (), s32[]{:S(2)}) async-start(), calls=%async_computation.4 | async-start | bytes 1064960
  564.4 3.3 copy-start.9
  564.4 3.3 copy-start.32
  571.7 2.6 copy-start.84
  578.2 2.7 copy-start.80
  580.9 1.5 copy-start.19
  582.4 1.5 copy-start.8
  582.4 1.5 copy-start.44
  583.9 1.5 copy-start.30
  589.4 2.6 copy-start.82
  595.9 2.7 copy-start.76
  598.7 1.5 copy-start.21
  600.1 1.4 copy-start.42
  601.6 1.5 copy-start.27
  607.1 2.6 copy-start.78
  613.6 2.7 copy-start.74
  616.4 1.5 copy-start.17
  621.9 2.6 copy-start.70
  631.0 2.6 copy-start.72
  652.2 2.6 copy-start.4
  654.8 2.2 copy-start.68
  663.2 1.6 copy-start.96
  663.3 1.6 copy-start.100
  663.3 1.6 copy-start.108
  665.7 1.8 copy-start.24
  666.8 5.7 copy-start.91
  671.4 281.7 %reduce-scatter.12.cloned.1.call-start = ((), (), s32[]{:S(2)}) async-start(), calls=%async_computation.5 | async-start | bytes 1064960
  676.4 419.0 %reduce-scatter.14.cloned.1.call-start = ((), (), s32[]{:S(2)}) async-start(), calls=%async_computation.6 | async-start | bytes 1064960
  (68 other events, 67.8 us)
Sparse Core Ops, SparseCore 0:
  134.1 191.7 all-reduce.7
  371.8 192.5 all-reduce.5
  671.5 139.1 reduce-scatter.9
  814.5 138.5 reduce-scatter.11
  956.9 138.4 reduce-scatter.13
